TPU v7x, 32 devices: a whole 2x2x4 slice. The times are simulated.
32 devices in a mesh: blk: 8 (over z, y), chan: 4 (over x, core).
Axes of the slice: x: 2, y: 2, z: 4, core: 2. Of those that a mesh axis runs over, the one named last changes fastest.
Arguments:
- hidden_in: bfloat16 [2, 1, 2048, 768], P(None, None, ('blk', 'chan')), may hold values from -6 to 6
- cotangent: bfloat16 [2, 1, 2048, 768], P(None, None, ('blk', 'chan')), may hold values from -6 to 6
- mixer_input_weight: bfloat16 [768, 2304], P(None, ('blk', 'chan')), may hold values from -0.21875 to 0.21875
- mixer_output_weight: bfloat16 [768, 768], P(None, ('blk', 'chan')), may hold values from -0.21875 to 0.21875
- feedforward_up: bfloat16 [768, 3072], P(None, ('blk', 'chan')), may hold values from -0.21875 to 0.21875
- feedforward_down: bfloat16 [3072, 768], P(('blk', 'chan')), may hold values from -0.109375 to 0.109375
- first_gain: bfloat16 [768], P(('blk', 'chan')), may hold values from 0.5 to 1.5
- first_shift: bfloat16 [768], P(('blk', 'chan')), may hold values from -3 to 3
- second_gain: bfloat16 [768], P(('blk', 'chan')), may hold values from 0.5 to 1.5
- second_shift: bfloat16 [768], P(('blk', 'chan')), may hold values from -3 to 3
- short_taps: bfloat16 [3, 3, 768], P(None, None, ('blk', 'chan')), may hold values from -4 to 4
- short_bias: bfloat16 [3, 768], P(None, ('blk', 'chan')), may hold values from -3 to 3
- skip_scale: bfloat16 [768], P(('blk', 'chan')), may hold values from -4 to 4
- filter_out: bfloat16 [64, 768], P(None, ('blk', 'chan')), may hold values from -0.023925781 to 0.023925781
- pos_weight: bfloat16 [33, 64], replicated, may hold values from -1 to 1
- pos_bias: bfloat16 [64], replicated, may hold values from -4 to 4
- mid_weight: bfloat16 [64, 64], replicated, may hold values from -0.75 to 0.75
- mid_bias: bfloat16 [64], replicated, may hold values from -4 to 4
- sine_freq: bfloat16 [64], replicated, may hold values from 2 to 16
- decay_rate: bfloat16 [768], P(('blk', 'chan')), may hold values from 0.00024414062 to 0.029907227
Outputs:
- hidden_out: bfloat16 [2, 1, 2048, 768], P(None, None, ('blk', 'chan'))
- grad_hidden: bfloat16 [2, 1, 2048, 768], P(None, None, ('blk', 'chan'))
- grad_mixer_in: float32 [768, 2304], P(None, ('blk', 'chan'))
- grad_mixer_out: float32 [768, 768], P(None, ('blk', 'chan'))
- grad_mlp_up: float32 [768, 3072], P(None, ('blk', 'chan'))
- grad_mlp_down: float32 [3072, 768], P(('blk', 'chan'))
- grad_first_gain: float32 [768], P(('blk', 'chan'))
- grad_first_shift: float32 [768], P(('blk', 'chan'))
- grad_second_gain: float32 [768], P(('blk', 'chan'))
- grad_second_shift: float32 [768], P(('blk', 'chan'))
- grad_short_taps: float32 [3, 3, 768], P(None, None, ('blk', 'chan'))
- grad_short_bias: float32 [3, 768], P(None, ('blk', 'chan'))
- grad_skip_scale: float32 [768], P(('blk', 'chan'))
- grad_filter_out: float32 [64, 768], P(None, ('blk', 'chan'))
- grad_pos_weight: float32 [33, 64], replicated
- grad_pos_bias: float32 [64], replicated
- grad_mid_weight: float32 [64, 64], replicated
- grad_mid_bias: float32 [64], replicated
- grad_sine_freq: float32 [64], replicated
All inputs are finite; a program needn't handle non-finite values.
Results may differ from a plain program's by a relative error of at most 0.012.
Values may be sent and summed in bfloat16 or wider, within the bound.
A program may use at most 320 MiB of HBM per device.

v0:
```python
import math

import jax
import jax.numpy as jnp
from jax import lax
from jax.sharding import PartitionSpec as P

BANDS = 16


EPS = 1e-05
PRECISION_LEVEL = lax.Precision.HIGHEST


def passed_along(value, axis, steps):
    count = lax.axis_size(axis)
    initial, last = (max(0, -steps), min(count, count - steps))
    return lax.ppermute(value, axis, [(source, source + steps) for source in range(initial, last)])


def positions(lags, length):
    band_freq = 0.0001 + (BANDS - 1 - 0.0001) * jnp.arange(BANDS).astype(jnp.float32) / (BANDS - 1)
    phase = 2.0 * math.pi / length * lags[:, None] * band_freq[None, :]
    return jnp.concatenate([lags[:, None] / (length - 1), jnp.cos(phase), -jnp.sin(phase)], 1)


def filter_values(lags, length, params, decay_rates):
    first_w, first_b, middle_w, middle_b, final_w, sine_rate = params
    layer_one = jnp.sin(
        sine_rate * (jnp.dot(positions(lags, length), first_w, precision=PRECISION_LEVEL) + first_b)
    )
    layer_two = jnp.sin(
        sine_rate * (jnp.dot(layer_one, middle_w, precision=PRECISION_LEVEL) + middle_b)
    )
    return jnp.dot(layer_two, final_w, precision=PRECISION_LEVEL) * jnp.exp(
        -lags[:, None] * decay_rates
    )


def norm_apply(values, gain, shift):
    center = values - jnp.mean(values, -1, keepdims=True)
    scale_inv = lax.rsqrt(jnp.mean(center * center, -1, keepdims=True) + EPS)
    normal = center * scale_inv
    return (normal * gain + shift, normal, scale_inv)


def norm_back(grad_out, normal, scale_inv, gain):
    grad_normal = grad_out * gain
    inner_term = grad_normal - jnp.mean(grad_normal, -1, keepdims=True)
    inner_term = inner_term - normal * jnp.mean(grad_normal * normal, -1, keepdims=True)
    return (inner_term * scale_inv, jnp.sum(grad_out * normal, (0, 1)), jnp.sum(grad_out, (0, 1)))


def gelu_tanh(values):
    return jax.nn.gelu(values, approximate=True)


def dft_tables(block_len):
    size_two = 2 * block_len
    freq_idx = lax.broadcasted_iota(jnp.int32, (block_len, size_two), 0)
    spot_idx = lax.broadcasted_iota(jnp.int32, (block_len, size_two), 1)
    phase = 2.0 * math.pi / size_two * (freq_idx * spot_idx % size_two).astype(jnp.float32)
    parity = lax.broadcasted_iota(jnp.int32, (size_two,), 0) % 2
    alternate = 1.0 - 2.0 * parity.astype(jnp.float32)
    weighting = (
        jnp.where(lax.broadcasted_iota(jnp.int32, (block_len,), 0) == 0, 1.0, 2.0) / size_two
    )
    return (jnp.cos(phase), jnp.sin(phase), alternate, weighting)


def output_tables(tables):
    cos_tab, sin_tab, alternate, weighting = tables
    block_len = cos_tab.shape[0]
    cos_out = cos_tab[:, block_len - 1 : 2 * block_len - 1] * weighting[:, None]
    sin_out = sin_tab[:, block_len - 1 : 2 * block_len - 1] * weighting[:, None]
    return (cos_out, sin_out, alternate[block_len - 1 : 2 * block_len - 1] / (2 * block_len))


def signal_spectrum(signal, tables):
    cos_tab, sin_tab, alternate, _ = tables
    block_len = signal.shape[1]
    real_part = jnp.einsum("fn,snc->fsc", cos_tab[:, :block_len], signal, precision=PRECISION_LEVEL)
    imag_part = -jnp.einsum(
        "fn,snc->fsc", sin_tab[:, :block_len], signal, precision=PRECISION_LEVEL
    )
    nyquist = jnp.einsum("n,snc->sc", alternate[:block_len], signal, precision=PRECISION_LEVEL)
    return (real_part, imag_part, nyquist)


def signal_adjoint(spectrum, tables):
    cos_tab, sin_tab, alternate, _ = tables
    real_part, imag_part, nyquist = spectrum
    block_len = cos_tab.shape[0]
    values = jnp.einsum("fn,fsc->snc", cos_tab[:, :block_len], real_part, precision=PRECISION_LEVEL)
    values = values - jnp.einsum(
        "fn,fsc->snc", sin_tab[:, :block_len], imag_part, precision=PRECISION_LEVEL
    )
    return values + alternate[:block_len][None, :, None] * nyquist[:, None, :]


def spectrum_output(spectrum, out_tabs):
    cos_out, sin_out, alt_out = out_tabs
    real_part, imag_part, nyquist = spectrum
    values = jnp.einsum("fn,fsc->snc", cos_out, real_part, precision=PRECISION_LEVEL)
    values = values - jnp.einsum("fn,fsc->snc", sin_out, imag_part, precision=PRECISION_LEVEL)
    return values + alt_out[None, :, None] * nyquist[:, None, :]


def output_adjoint(grad_values, out_tabs):
    cos_out, sin_out, alt_out = out_tabs
    real_part = jnp.einsum("fn,snc->fsc", cos_out, grad_values, precision=PRECISION_LEVEL)
    imag_part = -jnp.einsum("fn,snc->fsc", sin_out, grad_values, precision=PRECISION_LEVEL)
    nyquist = jnp.einsum("n,snc->sc", alt_out, grad_values, precision=PRECISION_LEVEL)
    return (real_part, imag_part, nyquist)


def segment_kernel(params, distance, block_len, length, decay_rates):
    size_two = 2 * block_len
    offset = lax.broadcasted_iota(jnp.int32, (size_two,), 0)
    lag_index = distance * block_len - (block_len - 1) + offset
    valid = jnp.logical_and(lag_index >= 0, offset < size_two - 1).astype(jnp.float32)
    lags = jnp.maximum(lag_index, 0).astype(jnp.float32)
    return filter_values(lags, length, params, decay_rates) * valid[:, None]


def kernel_spectrum(kernel, tables):
    cos_tab, sin_tab, alternate, _ = tables
    return (
        jnp.dot(cos_tab, kernel, precision=PRECISION_LEVEL),
        -jnp.dot(sin_tab, kernel, precision=PRECISION_LEVEL),
        jnp.dot(alternate, kernel, precision=PRECISION_LEVEL),
    )


def kernel_adjoint(spectrum, tables):
    cos_tab, sin_tab, alternate, _ = tables
    real_part, imag_part, nyquist = spectrum
    values = jnp.einsum("fm,fc->mc", cos_tab, real_part, precision=PRECISION_LEVEL)
    values = values - jnp.einsum("fm,fc->mc", sin_tab, imag_part, precision=PRECISION_LEVEL)
    return values + alternate[:, None] * nyquist[None, :]


def times_kernel(spectrum, kernel_spec):
    sig_re, sig_im, sig_ny = spectrum
    ker_re, ker_im, ker_ny = kernel_spec
    return (
        sig_re * ker_re[:, None] - sig_im * ker_im[:, None],
        sig_re * ker_im[:, None] + sig_im * ker_re[:, None],
        sig_ny * ker_ny[None],
    )


def adjoint_kernel(grad_spec, kernel_spec):
    grad_re, grad_im, grad_ny = grad_spec
    ker_re, ker_im, ker_ny = kernel_spec
    return (
        grad_re * ker_re[:, None] + grad_im * ker_im[:, None],
        grad_im * ker_re[:, None] - grad_re * ker_im[:, None],
        grad_ny * ker_ny[None],
    )


def adjoint_signal(grad_spec, signal_spec):
    grad_re, grad_im, grad_ny = grad_spec
    sig_re, sig_im, sig_ny = signal_spec
    return (
        jnp.sum(grad_re * sig_re + grad_im * sig_im, 1),
        jnp.sum(grad_im * sig_re - grad_re * sig_im, 1),
        jnp.sum(grad_ny * sig_ny, 0),
    )


def add_tuple(left_side, right_side):
    return tuple((lhs_val + rhs_val for lhs_val, rhs_val in zip(left_side, right_side)))


def keep_same(held_sum):
    return held_sum


def long_forward(gated_signal, kernel_at, tables, own_index):
    block_len = gated_signal.shape[1]
    spec_shape = (block_len, gated_signal.shape[0], gated_signal.shape[2])
    zero_spec = (
        jnp.zeros(spec_shape, jnp.float32),
        jnp.zeros(spec_shape, jnp.float32),
        jnp.zeros((gated_signal.shape[0], gated_signal.shape[2]), jnp.float32),
    )

    def pair_term(running, distance, spectrum):
        return add_tuple(running, times_kernel(spectrum, kernel_at(distance)))

    own_spec = signal_spectrum(gated_signal, tables)

    def visit_piece(running, piece, begin_at):

        def visit_block(inner_sum, element):
            block_index, spec_re, spec_im, spec_ny = element
            distance = own_index - block_index
            updated = lax.cond(
                distance >= 0,
                lambda held_sum: pair_term(held_sum, distance, (spec_re, spec_im, spec_ny)),
                keep_same,
                inner_sum,
            )
            return (updated, None)

        indices = jnp.arange(piece[0].shape[0], dtype=jnp.int32)
        result, _ = lax.scan(visit_block, running, (indices, piece[0], piece[1], piece[2]))
        return result

    summed = visit_piece(
        zero_spec,
        (
            lax.all_gather(
                own_spec[0][None].astype(jnp.bfloat16), "blk", axis=0, tiled=True
            ).astype(jnp.float32),
            lax.all_gather(
                own_spec[1][None].astype(jnp.bfloat16), "blk", axis=0, tiled=True
            ).astype(jnp.float32),
            lax.all_gather(
                own_spec[2][None].astype(jnp.bfloat16), "blk", axis=0, tiled=True
            ).astype(jnp.float32),
        ),
        jnp.int32(0),
    )
    return spectrum_output(summed, output_tables(tables))


def long_backward(
    grad_long, gated_signal, params, decay_rates, kernel_at, tables, length, own_index
):
    block_len = gated_signal.shape[1]
    out_tabs = output_tables(tables)
    own_grad = output_adjoint(grad_long, out_tabs)

    def filter_term(running, distance, signal_spec):
        kernel_grad = kernel_adjoint(adjoint_signal(own_grad, signal_spec), tables)
        _, pullback = jax.vjp(
            lambda weights: segment_kernel(weights, distance, block_len, length, decay_rates),
            params,
        )
        return (running[0], add_tuple(running[1], pullback(kernel_grad)[0]))

    def input_term(running, distance, grad_spec):
        return (add_tuple(running[0], adjoint_kernel(grad_spec, kernel_at(distance))), running[1])

    zero_state = (
        tuple((jnp.zeros_like(member) for member in own_grad)),
        tuple((jnp.zeros_like(member) for member in params)),
    )
    own_spec = signal_spectrum(gated_signal, tables)

    def visit_piece(running, piece, begin_at):

        def visit_block(inner_sum, element):
            block_index = element[0]
            signal_spec = element[1:4]
            grad_spec = element[4:7]
            inner_sum = lax.cond(
                block_index <= own_index,
                lambda held_sum: filter_term(held_sum, own_index - block_index, signal_spec),
                keep_same,
                inner_sum,
            )
            inner_sum = lax.cond(
                block_index >= own_index,
                lambda held_sum: input_term(held_sum, block_index - own_index, grad_spec),
                keep_same,
                inner_sum,
            )
            return (inner_sum, None)

        indices = jnp.arange(piece[0].shape[0], dtype=jnp.int32)
        result, _ = lax.scan(visit_block, running, (indices,) + tuple(piece))
        return result

    summed = visit_piece(
        zero_state,
        (
            lax.all_gather(
                own_spec[0][None].astype(jnp.bfloat16), "blk", axis=0, tiled=True
            ).astype(jnp.float32),
            lax.all_gather(
                own_spec[1][None].astype(jnp.bfloat16), "blk", axis=0, tiled=True
            ).astype(jnp.float32),
            lax.all_gather(
                own_spec[2][None].astype(jnp.bfloat16), "blk", axis=0, tiled=True
            ).astype(jnp.float32),
            lax.all_gather(
                own_grad[0][None].astype(jnp.bfloat16), "blk", axis=0, tiled=True
            ).astype(jnp.float32),
            lax.all_gather(
                own_grad[1][None].astype(jnp.bfloat16), "blk", axis=0, tiled=True
            ).astype(jnp.float32),
            lax.all_gather(
                own_grad[2][None].astype(jnp.bfloat16), "blk", axis=0, tiled=True
            ).astype(jnp.float32),
        ),
        jnp.int32(0),
    )
    spec_sum, param_grads = summed
    return (signal_adjoint(spec_sum, tables), param_grads)


def to_channels(values):
    return lax.all_to_all(values, "chan", split_axis=3, concat_axis=1, tiled=True)


def to_tokens(values):
    return lax.all_to_all(values, "chan", split_axis=1, concat_axis=3, tiled=True)


def shards(
    hidden_in,
    cotangent,
    mixer_input_weight,
    mixer_output_weight,
    feedforward_up,
    feedforward_down,
    first_gain,
    first_shift,
    second_gain,
    second_shift,
    short_taps,
    short_bias,
    skip_scale,
    filter_out,
    pos_weight,
    pos_bias,
    mid_weight,
    mid_bias,
    sine_freq,
    decay_rate,
):
    chan_count = lax.axis_size("chan")
    blk_count = lax.axis_size("blk")
    micro_count, seq_count, tok_count, model_width = hidden_in.shape
    block_len = tok_count * chan_count
    length = block_len * blk_count
    chan_width = model_width // chan_count
    own_index = lax.axis_index("blk")
    chan_start = lax.axis_index("chan") * chan_width
    tables = dft_tables(block_len)
    filter_head = tuple(
        (member.astype(jnp.float32) for member in (pos_weight, pos_bias, mid_weight, mid_bias))
    )
    freq_local = sine_freq.astype(jnp.float32)

    def fetch_weights():
        return (
            lax.all_gather(mixer_input_weight, ("blk", "chan"), axis=1, tiled=True),
            lax.all_gather(mixer_output_weight, ("blk", "chan"), axis=1, tiled=True),
            lax.all_gather(feedforward_up, ("blk", "chan"), axis=1, tiled=True),
            lax.all_gather(feedforward_down, ("blk", "chan"), axis=0, tiled=True),
            lax.all_gather(first_gain, ("blk", "chan"), axis=0, tiled=True),
            lax.all_gather(first_shift, ("blk", "chan"), axis=0, tiled=True),
            lax.all_gather(second_gain, ("blk", "chan"), axis=0, tiled=True),
            lax.all_gather(second_shift, ("blk", "chan"), axis=0, tiled=True),
            lax.all_gather(short_taps, ("blk", "chan"), axis=2, tiled=True),
            lax.all_gather(short_bias, ("blk", "chan"), axis=1, tiled=True),
            lax.all_gather(skip_scale, ("blk", "chan"), axis=0, tiled=True),
            lax.all_gather(filter_out, ("blk", "chan"), axis=1, tiled=True),
            lax.all_gather(decay_rate, ("blk", "chan"), axis=0, tiled=True),
        )

    def own_chans(values, axis):
        return lax.dynamic_slice_in_dim(values.astype(jnp.float32), chan_start, chan_width, axis)

    def spread_chans(values, axis, full_shape):
        return lax.dynamic_update_slice_in_dim(
            jnp.zeros(full_shape, jnp.float32), values, chan_start, axis
        )

    totals = None
    outputs = []
    input_grads = []
    for micro in range(micro_count):
        gathered = fetch_weights()
        weight_in, weight_out, weight_up, weight_down = (
            gathered[0],
            gathered[1],
            gathered[2],
            gathered[3],
        )
        gain_one = gathered[4].astype(jnp.float32)
        shift_one = gathered[5].astype(jnp.float32)
        gain_two = gathered[6].astype(jnp.float32)
        shift_two = gathered[7].astype(jnp.float32)
        taps = own_chans(gathered[8], 2)
        conv_bias = own_chans(gathered[9], 1)
        skip_local = own_chans(gathered[10], 0)
        filter_params = filter_head + (own_chans(gathered[11], 1), freq_local)
        decay_local = own_chans(gathered[12], 0)

        def build_spectrum(distance, weights_now=filter_params, decay_now=decay_local):
            return kernel_spectrum(
                segment_kernel(weights_now, distance, block_len, length, decay_now), tables
            )

        values = hidden_in[micro].astype(jnp.float32)
        normalized_input, first_normal, first_inv = norm_apply(values, gain_one, shift_one)
        normed_low = normalized_input.astype(jnp.bfloat16)
        projected_tokens = jnp.dot(
            normed_low, weight_in, preferred_element_type=jnp.float32
        ).astype(jnp.bfloat16)
        grouped = to_channels(projected_tokens.reshape(seq_count, tok_count, 3, model_width))
        prior = passed_along(grouped[:, -2:], "blk", 1)
        extended = jnp.concatenate([prior, grouped], 1).astype(jnp.float32)
        conv = (
            taps[0] * extended[:, 2:]
            + taps[1] * extended[:, 1:-1]
            + taps[2] * extended[:, :-2]
            + conv_bias
        )
        gate_out = conv[:, :, 0]
        gate_in = conv[:, :, 1]
        signal = conv[:, :, 2]
        gated_signal = signal * gate_in
        long_out = long_forward(gated_signal, build_spectrum, tables, own_index)
        long_total = long_out + skip_local * gated_signal
        mixed_low = (long_total * gate_out).astype(jnp.bfloat16)
        mixed_tokens = to_tokens(mixed_low[:, :, None, :]).reshape(
            seq_count, tok_count, model_width
        )
        residual_stream = values + jnp.dot(
            mixed_tokens, weight_out, preferred_element_type=jnp.float32
        )
        second_branch, second_normal, second_inv = norm_apply(residual_stream, gain_two, shift_two)
        second_low = second_branch.astype(jnp.bfloat16)
        upper_branch = jnp.dot(second_low, weight_up, preferred_element_type=jnp.float32)
        activated_hidden, gelu_pull = jax.vjp(gelu_tanh, upper_branch)
        active_low = activated_hidden.astype(jnp.bfloat16)
        result = residual_stream + jnp.dot(
            active_low, weight_down, preferred_element_type=jnp.float32
        )
        outputs.append(result.astype(jnp.bfloat16))
        back_weights = fetch_weights()
        weight_in, weight_out, weight_up, weight_down = (
            back_weights[0],
            back_weights[1],
            back_weights[2],
            back_weights[3],
        )
        grad_low = cotangent[micro]
        grad_down_w = jnp.einsum(
            "sti,sto->io", active_low, grad_low, preferred_element_type=jnp.float32
        )
        grad_active = jnp.einsum(
            "sto,io->sti", grad_low, weight_down, preferred_element_type=jnp.float32
        )
        grad_upper_low = gelu_pull(grad_active)[0].astype(jnp.bfloat16)
        grad_up_w = jnp.einsum(
            "std,ste->de", second_low, grad_upper_low, preferred_element_type=jnp.float32
        )
        grad_second = jnp.einsum(
            "ste,de->std", grad_upper_low, weight_up, preferred_element_type=jnp.float32
        )
        resid_term, grad_gain_two, grad_shift_two = norm_back(
            grad_second, second_normal, second_inv, gain_two
        )
        grad_resid = grad_low.astype(jnp.float32) + resid_term
        grad_branch_low = grad_resid.astype(jnp.bfloat16)
        grad_out_w = jnp.einsum(
            "std,ste->de", mixed_tokens, grad_branch_low, preferred_element_type=jnp.float32
        )
        grad_mixed_tok = jnp.einsum(
            "ste,de->std", grad_branch_low, weight_out, preferred_element_type=jnp.float32
        ).astype(jnp.bfloat16)
        grad_mixed = to_channels(grad_mixed_tok[:, :, None, :])[:, :, 0].astype(jnp.float32)
        grad_gate_out = grad_mixed * long_total
        grad_long = grad_mixed * gate_out
        grad_skip = jnp.sum(grad_long * gated_signal, (0, 1))
        grad_from_long, filter_grads = long_backward(
            grad_long,
            gated_signal,
            filter_params,
            decay_local,
            build_spectrum,
            tables,
            length,
            own_index,
        )
        grad_gated = grad_from_long + grad_long * skip_local
        grad_conv = jnp.stack([grad_gate_out, grad_gated * signal, grad_gated * gate_in], 2)
        grad_bias = jnp.sum(grad_conv, (0, 1))
        grad_taps = jnp.stack(
            [
                jnp.sum(grad_conv * extended[:, 2:], (0, 1)),
                jnp.sum(grad_conv * extended[:, 1:-1], (0, 1)),
                jnp.sum(grad_conv * extended[:, :-2], (0, 1)),
            ]
        )
        spill = jnp.stack(
            [taps[2] * grad_conv[:, 0], taps[1] * grad_conv[:, 0] + taps[2] * grad_conv[:, 1]], 1
        )
        returned = passed_along(spill, "blk", -1)
        padded_grad = jnp.concatenate([grad_conv, jnp.zeros_like(grad_conv[:, :2])], 1)
        grad_grouped = (
            taps[0] * grad_conv + taps[1] * padded_grad[:, 1:-1] + taps[2] * padded_grad[:, 2:]
        )
        grad_grouped = jnp.concatenate([grad_grouped[:, :-2], grad_grouped[:, -2:] + returned], 1)
        grad_proj = to_tokens(grad_grouped.astype(jnp.bfloat16)).reshape(
            seq_count, tok_count, 3 * model_width
        )
        grad_in_w = jnp.einsum(
            "std,ste->de", normed_low, grad_proj, preferred_element_type=jnp.float32
        )
        grad_normed = jnp.einsum(
            "ste,de->std", grad_proj, weight_in, preferred_element_type=jnp.float32
        )
        input_term, grad_gain_one, grad_shift_one = norm_back(
            grad_normed, first_normal, first_inv, gain_one
        )
        input_grads.append((grad_resid + input_term).astype(jnp.bfloat16))
        micro_grads = (
            grad_in_w,
            grad_out_w,
            grad_up_w,
            grad_down_w,
            grad_gain_one,
            grad_shift_one,
            grad_gain_two,
            grad_shift_two,
            spread_chans(grad_taps, 2, (3, 3, model_width)),
            spread_chans(grad_bias, 1, (3, model_width)),
            spread_chans(grad_skip, 0, (model_width,)),
            spread_chans(filter_grads[4], 1, (filter_grads[4].shape[0], model_width)),
            filter_grads[0],
            filter_grads[1],
            filter_grads[2],
            filter_grads[3],
            filter_grads[5],
        )
        totals = micro_grads if totals is None else add_tuple(totals, micro_grads)
    weight_grads = (
        lax.psum_scatter(totals[0], ("blk", "chan"), scatter_dimension=1, tiled=True),
        lax.psum_scatter(totals[1], ("blk", "chan"), scatter_dimension=1, tiled=True),
        lax.psum_scatter(totals[2], ("blk", "chan"), scatter_dimension=1, tiled=True),
        lax.psum_scatter(totals[3], ("blk", "chan"), scatter_dimension=0, tiled=True),
        lax.psum_scatter(totals[4], ("blk", "chan"), scatter_dimension=0, tiled=True),
        lax.psum_scatter(totals[5], ("blk", "chan"), scatter_dimension=0, tiled=True),
        lax.psum_scatter(totals[6], ("blk", "chan"), scatter_dimension=0, tiled=True),
        lax.psum_scatter(totals[7], ("blk", "chan"), scatter_dimension=0, tiled=True),
        lax.psum_scatter(totals[8], ("blk", "chan"), scatter_dimension=2, tiled=True),
        lax.psum_scatter(totals[9], ("blk", "chan"), scatter_dimension=1, tiled=True),
        lax.psum_scatter(totals[10], ("blk", "chan"), scatter_dimension=0, tiled=True),
        lax.psum_scatter(totals[11], ("blk", "chan"), scatter_dimension=1, tiled=True),
    )
    small_grads = lax.psum(
        (totals[12], totals[13], totals[14], totals[15], totals[16]), ("blk", "chan")
    )
    return (
        jnp.stack(outputs),
        jnp.stack(input_grads),
        weight_grads[0],
        weight_grads[1],
        weight_grads[2],
        weight_grads[3],
        weight_grads[4],
        weight_grads[5],
        weight_grads[6],
        weight_grads[7],
        weight_grads[8],
        weight_grads[9],
        weight_grads[10],
        weight_grads[11],
        small_grads[0],
        small_grads[1],
        small_grads[2],
        small_grads[3],
        small_grads[4],
    )


def solution(mesh):
    return jax.shard_map(
        shards,
        mesh=mesh,
        in_specs=(
            P(None, None, ("blk", "chan"), None),
            P(None, None, ("blk", "chan"), None),
            P(None, ("blk", "chan")),
            P(None, ("blk", "chan")),
            P(None, ("blk", "chan")),
            P(("blk", "chan"), None),
            P(("blk", "chan")),
            P(("blk", "chan")),
            P(("blk", "chan")),
            P(("blk", "chan")),
            P(None, None, ("blk", "chan")),
            P(None, ("blk", "chan")),
            P(("blk", "chan")),
            P(None, ("blk", "chan")),
            P(),
            P(),
            P(),
            P(),
            P(),
            P(("blk", "chan")),
        ),
        out_specs=(
            P(None, None, ("blk", "chan"), None),
            P(None, None, ("blk", "chan"), None),
            P(None, ("blk", "chan")),
            P(None, ("blk", "chan")),
            P(None, ("blk", "chan")),
            P(("blk", "chan"), None),
            P(("blk", "chan")),
            P(("blk", "chan")),
            P(("blk", "chan")),
            P(("blk", "chan")),
            P(None, None, ("blk", "chan")),
            P(None, ("blk", "chan")),
            P(("blk", "chan")),
            P(None, ("blk", "chan")),
            P(),
            P(),
            P(),
            P(),
            P(),
        ),
        check_vma=False,
    )
```

profile of v0, /device:TPU:0, one launch (start us, length us, event | category | flops | bytes accessed | tf_op | source)
XLA Modules:
  0.0 2056.0 jit_solution(5179023431376144872)
XLA Ops:
  20.3 42.4 %all-reduce.21 = (bf16[768]{0:T(1024)(128)(2,1)S(1)}, bf16[768]{0:T(1024)(128)(2,1)S(1)}, bf16[768]{0:T(1024)(128)(2,1)}, bf16[768]{0:T(1024)(128)(2,1)}, bf16[768]{0:T(1024)(128)(2,1)}, /*index=5*/bf16[768]{0:T(1024)(128)(2,1)}) all-reduce(bf16[768]{0:T(1024)(128)(2,1)S(1)} %dynamic-update-slice.5, ...), channel_id=1, replica_groups=mesh['blk'=8,'chan'=4] {'blk','chan'}, use_global_device_ids=true, to_apply=%add.3 | all-reduce | flops 4608 | bytes 18432
  65.1 41.0 %all-gather.12 = bf16[32,24,3]{1,2,0:T(4,128)(2,1)S(1)} all-gather(bf16[1,24,3]{1,2,0:T(4,128)(2,1)} %bitcast.834), channel_id=1, replica_groups=mesh['blk'=8,'chan'=4] {'blk','chan'}, dimensions={0}, use_global_device_ids=true | all-gather | bytes 4752 | tf_op jit(solution)/shard_map/all_gather | solution.py:361
  107.7 39.2 %all_gather.50 = bf16[3,3,768]{1,0,2:T(4,128)(2,1)S(1)} all-gather(bf16[3,3,24]{1,0,2:T(4,128)(2,1)S(1)} %copy.631), channel_id=1, replica_groups=mesh['blk'=8,'chan'=4] {'blk','chan'}, dimensions={2}, use_global_device_ids=true | all-gather | bytes 14256 | tf_op jit(solution)/shard_map/all_gather | solution.py:360
  148.3 38.9 %all_gather.108 = bf16[64,768]{0,1:T(8,128)(2,1)S(1)} all-gather(bf16[64,24]{0,1:T(8,128)(2,1)S(1)} %copy-done.106), channel_id=1, replica_groups=mesh['blk'=8,'chan'=4] {'blk','chan'}, dimensions={1}, use_global_device_ids=true | all-gather | bytes 101376 | tf_op jit(solution)/shard_map/all_gather | solution.py:363
  188.5 4.0 convolution_convert_fusion.1
  199.0 4.1 all-to-all-start
  210.6 3.5 all-to-all-start.2
  226.0 3.4 collective-permute-done.1
  231.4 36.8 %all-gather.3 = bf16[2048,192]{0,1:T(8,128)(2,1)S(1)} all-gather(bf16[256,192]{0,1:T(8,128)(2,1)S(1)} %convolution_convert_fusion.4), channel_id=5, replica_groups=mesh['blk'=8,'chan'=4] {'blk'}, dimensions={0}, use_global_device_ids=true | all-gather | bytes 884736 | tf_op jit(solution)/shard_map/all_gather | solution.py:215
  271.1 32.2 %all-gather.4 = bf16[2048,192]{0,1:T(8,128)(2,1)S(1)} all-gather(bf16[256,192]{0,1:T(8,128)(2,1)S(1)} %fusion.235), channel_id=6, replica_groups=mesh['blk'=8,'chan'=4] {'blk'}, dimensions={0}, use_global_device_ids=true | all-gather | bytes 884736 | tf_op jit(solution)/shard_map/all_gather | solution.py:218
  306.8 17.9 all-reduce.23
  324.9 22.5 %while.87 = (s32[]{:T(128)}, f32[256,1,192]{0,2,1:T(8,128)S(1)}, f32[256,1,192]{0,2,1:T(8,128)S(1)}, f32[1,192]{1,0:T(1,128)S(1)}, s32[8]{0:T(128)S(1)}, /*index...) while((s32[]{:T(128)}, f32[256,1,192]{0,2,1:T(8,128)S(1)}, ...), condition=%wide.region_13.14_spmd.clone, body=%wide.region_10.13_spmd.clone.sunk | while | flops 721564608 | bytes 5481799 | solution.py:209
  326.4 10.1 conditional.23
  332.4 3.6 bitcast_add_fusion.6
  353.4 3.9 all-to-all-start.3
  357.7 99.3 %all-gather = bf16[2048,192]{0,1:T(8,128)(2,1)S(1)} all-gather(bf16[256,192]{0,1:T(8,128)(2,1)S(1)} %convolution_convert_fusion.5), channel_id=2, replica_groups=mesh['blk'=8,'chan'=4] {'blk'}, dimensions={0}, use_global_device_ids=true | all-gather | bytes 884736 | tf_op jit(solution)/shard_map/all_gather | solution.py:215
  459.9 32.3 %all-gather.1 = bf16[2048,192]{0,1:T(8,128)(2,1)S(1)} all-gather(bf16[256,192]{0,1:T(8,128)(2,1)S(1)} %fusion.234), channel_id=3, replica_groups=mesh['blk'=8,'chan'=4] {'blk'}, dimensions={0}, use_global_device_ids=true | all-gather | bytes 884736 | tf_op jit(solution)/shard_map/all_gather | solution.py:218
  494.7 22.5 %while.86 = (s32[]{:T(128)}, f32[256,1,192]{0,2,1:T(8,128)S(1)}, f32[256,1,192]{0,2,1:T(8,128)S(1)}, f32[1,192]{1,0:T(1,128)S(1)}, s32[8]{0:T(128)S(1)}, /*index...) while((s32[]{:T(128)}, f32[256,1,192]{0,2,1:T(8,128)S(1)}, ...), condition=%wide.region_5.6_spmd.clone, body=%wide.region_2.5_spmd.clone.sunk | while | flops 721564608 | bytes 5481799 | solution.py:209
  496.3 10.1 conditional.22
  502.3 3.6 bitcast_add_fusion.4
  522.8 3.6 all-to-all-start.1
  535.6 4.9 fusion.420
  542.8 4.5 fusion.253
  562.1 3.9 all-to-all-start.6
  572.6 4.3 all-to-all-start.4
  594.7 102.8 %all-gather.9 = bf16[2048,192]{0,1:T(8,128)(2,1)S(1)} all-gather(bf16[256,192]{0,1:T(8,128)(2,1)S(1)} %get-tuple-element.3563), channel_id=11, replica_groups=mesh['blk'=8,'chan'=4] {'blk'}, dimensions={0}, use_global_device_ids=true | all-gather | bytes 884736 | tf_op jit(solution)/shard_map/all_gather | solution.py:290
  700.0 32.1 %all-gather.10 = bf16[2048,192]{0,1:T(8,128)(2,1)S(1)} all-gather(bf16[256,192]{0,1:T(8,128)(2,1)S(1)} %get-tuple-element.3565), channel_id=12, replica_groups=mesh['blk'=8,'chan'=4] {'blk'}, dimensions={0}, use_global_device_ids=true | all-gather | bytes 884736 | tf_op jit(solution)/shard_map/all_gather | solution.py:293
  735.7 23.0 %all-reduce.22 = (bf16[1536]{0:T(1024)(128)(2,1)S(1)}, bf16[1536]{0:T(1024)(128)(2,1)}) all-reduce(bf16[1536]{0:T(1024)(128)(2,1)S(1)} %dynamic-update-slice.13, bf16[1536]{0:T(1024)(128)(2,1)S(1)} %dynamic-update-slice.12), channel_id=13, replica_groups=mesh['blk'=8,'chan'=4] {'blk'}, use_global_device_ids=true, to_apply=%add.11 | all-reduce | flops 3072 | bytes 12288
  764.6 136.9 %while.89 = (s32[]{:T(128)}, f32[256,1,192]{0,2,1:T(8,128)S(1)}, f32[256,1,192]{0,2,1:T(8,128)}, f32[1,192]{1,0:T(1,128)}, f32[33,64]{1,0:T(8,128)}, /*index=5*/...) while((s32[]{:T(128)}, f32[256,1,192]{0,2,1:T(8,128)S(1)}, ...), condition=%wide.region_41.42_spmd.clone.clone, body=%wide.region_32.41_spmd.clone.clone.sunk | while | flops 1579639040 | bytes 12768181 | solution.py:275
  768.7 10.0 conditional.26
  779.3 18.9 conditional.27
  802.3 10.0 conditional.26
  817.1 9.9 conditional.26
  831.8 10.0 conditional.26
  846.6 10.0 conditional.26
  861.3 10.0 conditional.26
  876.1 10.0 conditional.26
  890.8 10.0 conditional.26
  907.0 90.8 %all-gather.6 = bf16[2048,192]{0,1:T(8,128)(2,1)S(1)} all-gather(bf16[256,192]{0,1:T(8,128)(2,1)} %get-tuple-element.3559), channel_id=8, replica_groups=mesh['blk'=8,'chan'=4] {'blk'}, dimensions={0}, use_global_device_ids=true | all-gather | bytes 884736 | tf_op jit(solution)/shard_map/all_gather | solution.py:290
  1000.3 31.6 %all-gather.7 = bf16[2048,192]{0,1:T(8,128)(2,1)S(1)} all-gather(bf16[256,192]{0,1:T(8,128)(2,1)S(1)} %copy-done.58), channel_id=9, replica_groups=mesh['blk'=8,'chan'=4] {'blk'}, dimensions={0}, use_global_device_ids=true | all-gather | bytes 884736 | tf_op jit(solution)/shard_map/all_gather | solution.py:293
  1040.3 135.1 %while.88 = (s32[]{:T(128)}, f32[256,1,192]{0,2,1:T(8,128)S(1)}, f32[256,1,192]{0,2,1:T(8,128)}, f32[1,192]{1,0:T(1,128)}, f32[33,64]{1,0:T(8,128)}, /*index=5*/...) while((s32[]{:T(128)}, f32[256,1,192]{0,2,1:T(8,128)S(1)}, ...), condition=%wide.region_27.28_spmd.clone.clone, body=%wide.region_18.27_spmd.clone.clone.sunk | while | flops 1579639040 | bytes 12768181 | solution.py:275
  1044.3 9.9 conditional.24
  1054.8 19.1 conditional.25
  1077.8 9.8 conditional.24
  1092.3 9.8 conditional.24
  1106.7 9.9 conditional.24
  1121.2 9.9 conditional.24
  1135.7 9.9 conditional.24
  1150.2 9.9 conditional.24
  1164.7 9.9 conditional.24
  1203.3 3.5 all-to-all-start.7
  1208.9 6.7 all-to-all-done.7
  1215.5 4.1 all-to-all-start.5
  1224.3 4.3 all-to-all-done.5
  1239.8 3.7 convolution_add_fusion.21
  1245.8 4.1 convolution_add_fusion.18
  1252.5 5.2 convolution_add_fusion.20
  1260.4 5.1 convolution_add_fusion.19
  1274.0 156.0 %all-reduce.26.cloned.1.call-done = (f32[768]{0:T(1024)}, f32[768]{0:T(1024)}, f32[768]{0:T(1024)}, f32[768]{0:T(1024)}, f32[3,3,768]{2,1,0:T(4,128)}, /*index=5...) async-done(((f32[768]{0:T(1024)}, f32[768]{0:T(1024)}, f32[768]{0:T(1024)}, ...) | async-done | bytes 77840
  1439.0 91.3 %reduce-scatter.18.cloned.1.call-done = f32[64,24]{0,1:T(8,128)} async-done(((f32[64,768]{0,1:T(8,128)}), f32[64,24]{0,1:T(8,128)}) %reduce-scatter.18.cloned.1.call-update) | async-done | bytes 6160
  1530.4 104.0 %reduce-scatter.12.cloned.1.call-done = f32[768,24]{0,1:T(8,128)} async-done(((f32[768,768]{0,1:T(8,128)}), f32[768,24]{0,1:T(8,128)}) %reduce-scatter.12.cloned.1.call-update) | async-done | bytes 73744 | tf_op jit(solution)/shard_map/reduce_scatter | solution.py:538
  1634.4 125.4 %reduce-scatter.10.cloned.1.call-done = f32[768,72]{0,1:T(8,128)} async-done(((f32[768,2304]{0,1:T(8,128)}), f32[768,72]{0,1:T(8,128)}) %reduce-scatter.10.cloned.1.call-update) | async-done | bytes 221200 | tf_op jit(solution)/shard_map/reduce_scatter | solution.py:537
  1759.8 141.3 %reduce-scatter.14.cloned.1.call-done = f32[768,96]{0,1:T(8,128)} async-done(((f32[768,3072]{0,1:T(8,128)}), f32[768,96]{0,1:T(8,128)}) %reduce-scatter.14.cloned.1.call-update) | async-done | bytes 294928 | tf_op jit(solution)/shard_map/reduce_scatter | solution.py:539
  1901.1 141.7 %reduce-scatter.16.cloned.1.call-done = f32[96,768]{1,0:T(8,128)} async-done(((f32[3072,768]{1,0:T(8,128)}), f32[96,768]{1,0:T(8,128)}) %reduce-scatter.16.cloned.1.call-update) | async-done | bytes 294928 | tf_op jit(solution)/shard_map/reduce_scatter | solution.py:540
  (978 shorter events, 488.1 us)
Async XLA Ops:
  7.2 181.3 %copy-start.14 = (bf16[2,1,64,768]{3,2,1,0:T(8,128)(2,1)S(1)}, bf16[2,1,64,768]{3,2,1,0:T(8,128)(2,1)}, u32[]{:S(2)}) copy-start(bf16[2,1,64,768]{3,2,1,0:T(8,128)(2,1)} %param.40) | copy-start | bytes 589828
  7.2 141.1 %copy-start.106 = (bf16[64,24]{0,1:T(8,128)(2,1)S(1)}, bf16[64,24]{0,1:T(8,128)(2,1)}, u32[]{:S(2)}) copy-start(bf16[64,24]{0,1:T(8,128)(2,1)} %param.53) | copy-start | bytes 9220
  7.2 181.3 %all-gather.18.cloned.1.call-start = ((), (), s32[]{:S(2)}) async-start(), calls=%async_computation.13 | async-start | bytes 3649536 | tf_op jit(solution)/shard_map/all_gather | solution.py:352
  7.9 523.3 %all-gather.20.cloned.1.call-start = ((), (), s32[]{:S(2)}) async-start(), calls=%async_computation.14 | async-start | bytes 1216512 | tf_op jit(solution)/shard_map/all_gather | solution.py:353
  8.7 526.8 %all-gather.22.cloned.1.call-start = ((), (), s32[]{:S(2)}) async-start(), calls=%async_computation.15 | async-start | bytes 4866048 | tf_op jit(solution)/shard_map/all_gather | solution.py:354
  9.4 533.3 %all-gather.24.cloned.1.call-start = ((), (), s32[]{:S(2)}) async-start(), calls=%async_computation.16 | async-start | bytes 4866048 | tf_op jit(solution)/shard_map/all_gather | solution.py:355
  62.7 140.4 %copy-start.54 = (f32[768]{0:T(1024)}, f32[768]{0:T(1024)S(1)}, u32[]{:S(2)}) copy-start(f32[768]{0:T(1024)S(1)} %convert_element_type.808) | copy-start | bytes 9220
  63.8 124.6 %copy-start.89 = (f32[64]{0:T(128)}, f32[64]{0:T(128)S(1)}, u32[]{:S(2)}) copy-start(f32[64]{0:T(128)S(1)} %broadcast_multiply_fusion.11) | copy-start | bytes 772
  63.9 83.1 %copy-start.83 = (f32[64]{0:T(128)}, f32[64]{0:T(128)S(1)}, u32[]{:S(2)}) copy-start(f32[64]{0:T(128)S(1)} %broadcast_multiply_fusion.9) | copy-start | bytes 772
  65.0 123.4 %copy-start.99 = (f32[64]{0:T(128)}, f32[64]{0:T(128)S(1)}, u32[]{:S(2)}) copy-start(f32[64]{0:T(128)S(1)} %add_rsqrt_fusion.3) | copy-start | bytes 772
  147.2 47.3 %copy-start.61 = (bf16[3,3,192]{2,0,1:T(4,128)(2,1)}, bf16[3,3,192]{2,0,1:T(4,128)(2,1)S(1)}, u32[]{:S(2)}) copy-start(bf16[3,3,192]{2,0,1:T(4,128)(2,1)S(1)} %copy.698) | copy-start | bytes 10372
  192.4 10.7 copy-start.2
  199.0 11.6 all-to-all-start
  209.0 10.1 copy-start.116
  209.0 10.1 copy-start.105
  209.0 10.7 copy-start.117
  209.0 11.2 copy-start.92
  209.0 11.2 copy-start.118
  209.0 11.7 copy-start.59
  209.1 11.8 copy-start.115
  209.1 11.9 copy-start.119
  209.1 12.5 copy-start.114
  210.6 11.6 all-to-all-start.2
  217.7 8.1 collective-permute-start
  219.0 298.8 %copy-start.64 = (f32[256]{0:T(256)}, f32[256]{0:T(256)S(1)}, u32[]{:S(2)}) copy-start(f32[256]{0:T(256)S(1)} %fusion.415) | copy-start | bytes 3076
  219.0 10.6 copy-start.68
  219.0 10.6 copy-start.70
  219.1 10.6 copy-start.72
  221.6 296.1 %copy-start.80 = (f32[192]{0:T(256)}, f32[192]{0:T(256)S(1)}, u32[]{:S(2)}) copy-start(f32[192]{0:T(256)S(1)} %dynamic_slice.183) | copy-start | bytes 2308
  224.1 5.3 collective-permute-start.1
  230.7 75.1 %copy-start.25 = (f32[1,256,3,192]{1,3,2,0:T(8,128)}, f32[1,256,3,192]{1,3,2,0:T(8,128)S(1)}, u32[]{:S(2)}) copy-start(f32[1,256,3,192]{1,3,2,0:T(8,128)S(1)} %get-tuple-element.3540) | copy-start | bytes 1769476
  230.7 75.4 %copy-start.23 = (f32[1,256,3,192]{1,3,2,0:T(8,128)}, f32[1,256,3,192]{1,3,2,0:T(8,128)S(1)}, u32[]{:S(2)}) copy-start(f32[1,256,3,192]{1,3,2,0:T(8,128)S(1)} %get-tuple-element.3539) | copy-start | bytes 1769476
  324.9 23.0 %copy-start.78 = (f32[256]{0:T(256)S(1)}, f32[256]{0:T(256)}, u32[]{:S(2)}) copy-start(f32[256]{0:T(256)} %get-tuple-element.3552) | copy-start | bytes 3076
  347.4 109.7 %copy-start.67 = (f32[8,1,192]{2,1,0:T(1,128)}, f32[8,1,192]{2,1,0:T(1,128)S(1)}, u32[]{:S(2)}) copy-start(f32[8,1,192]{2,1,0:T(1,128)S(1)} %get-tuple-element.4610) | copy-start | bytes 18436
  349.4 107.9 %copy-start.39 = (f32[1,256,192]{1,2,0:T(8,128)}, f32[1,256,192]{1,2,0:T(8,128)S(1)}, u32[]{:S(2)}) copy-start(f32[1,256,192]{1,2,0:T(8,128)S(1)} %fusion.227) | copy-start | bytes 589828
  353.4 169.4 %all-to-all-start.3 = ((bf16[4,2,6144]{2,1,0:T(2,128)(2,1)}), bf16[4,2,6144]{2,1,0:T(2,128)(2,1)}, u32[]{:S(2)}, u32[]{:S(2)}) async-start(bf16[4,2,6144]{2,1,0:T(2,128)(2,1)} %reshape.1981), calls=%async_computation.3 | async-start | bytes 196608 | tf_op jit(solution)/shard_map/all_to_all | solution.py:311
  519.3 11.9 copy-start.38
  519.3 11.9 copy-start.15
  522.8 7.9 all-to-all-start.1
  533.1 19.4 copy-start.12
  533.1 19.4 copy-start.85
  535.2 17.3 copy-start.87
  535.5 17.1 copy-start.95
  535.5 17.1 copy-start.97
  552.5 13.5 copy-start.47
  553.5 12.6 copy-start.29
  562.1 10.5 all-to-all-start.6
  568.3 11.0 copy-start.65
  570.6 11.6 copy-start.79
  572.6 11.3 all-to-all-start.4
  589.7 145.5 %copy-start.74 = (f32[1,192]{1,0:T(1,128)}, f32[1,192]{1,0:T(1,128)S(1)}, u32[]{:S(2)}) copy-start(f32[1,192]{1,0:T(1,128)S(1)} %fusion.416) | copy-start | bytes 2308
  1040.3 135.2 %copy-start.9 = (f32[256,512]{1,0:T(8,128)S(1)}, f32[256,512]{1,0:T(8,128)}, u32[]{:S(2)}) copy-start(f32[256,512]{1,0:T(8,128)} %fusion.271) | copy-start | bytes 1572868
  1184.3 17.6 collective-permute-start.3
  1189.3 18.2 collective-permute-start.2
  1203.3 12.3 all-to-all-start.7
  1215.5 13.1 all-to-all-start.5
  1219.7 210.3 %all-reduce.26.cloned.1.call-start = ((), (), s32[]{:S(2)}) async-start(), calls=%async_computation.22 | async-start | bytes 248832
  1219.9 12.9 copy-start.82
  1219.9 12.9 copy-start.3
  1238.0 292.3 %reduce-scatter.18.cloned.1.call-start = ((), (), s32[]{:S(2)}) async-start(), calls=%async_computation.21 | async-start | bytes 405504
  1239.7 394.7 %reduce-scatter.12.cloned.1.call-start = ((), (), s32[]{:S(2)}) async-start(), calls=%async_computation.18 | async-start | bytes 2433024 | tf_op jit(solution)/shard_map/reduce_scatter | solution.py:538
  1243.6 516.2 %reduce-scatter.10.cloned.1.call-start = ((), (), s32[]{:S(2)}) async-start(), calls=%async_computation.17 | async-start | bytes 7299072 | tf_op jit(solution)/shard_map/reduce_scatter | solution.py:537
  1250.0 651.1 %reduce-scatter.14.cloned.1.call-start = ((), (), s32[]{:S(2)}) async-start(), calls=%async_computation.19 | async-start | bytes 9732096 | tf_op jit(solution)/shard_map/reduce_scatter | solution.py:539
  1257.8 785.0 %reduce-scatter.16.cloned.1.call-start = ((), (), s32[]{:S(2)}) async-start(), calls=%async_computation.20 | async-start | bytes 9732096 | tf_op jit(solution)/shard_map/reduce_scatter | solution.py:540
  (78 other events, 263.8 us)
Sparse Core Ops, SparseCore 0:
  10.9 63.1 all-gather.17
  77.0 53.9 all-gather.19
  133.9 62.0 all-gather.21
  198.8 72.9 all-gather.23
  1238.2 191.8 all-reduce.25
  1436.2 94.1 reduce-scatter.17
  1536.2 98.1 reduce-scatter.11
  1641.6 118.1 reduce-scatter.9
  1766.3 134.8 reduce-scatter.13
  1908.4 134.3 reduce-scatter.15
where the time goes:
time: 2070 us; the launch traced here: 2060 us
  waiting for transfers between devices  784 us (38%)
  blocking collectives  660 us (32%)
  matrix products  242 us (12%)
  local copies, waits for them, and re-layouts  152 us (7%)
  other arithmetic  117 us (6%)
  loops' own time  46.7 us (2%)
  starting transfers between devices  37.1 us (2%)
    unnamed x12, waiting for transfers between devices  250 us
    all_gather x2, blocking collectives, long_backward(): lax.all_gather(own_grad[0][None].astype(jnp.bfloat16), 'blk', axis=0, til...  194 us
    reduce_scatter x1, waiting for transfers between devices, shards(): lax.psum_scatter(totals[3], ('blk', 'chan'), scatter_dimension=0, tiled=T...  142 us
    reduce_scatter x1, waiting for transfers between devices, shards(): lax.psum_scatter(totals[2], ('blk', 'chan'), scatter_dimension=1, tiled=T...  141 us
    all_gather x2, blocking collectives, long_forward(): lax.all_gather(own_spec[0][None].astype(jnp.bfloat16), 'blk', axis=0, til...  136 us
    reduce_scatter x1, waiting for transfers between devices, shards(): lax.psum_scatter(totals[0], ('blk', 'chan'), scatter_dimension=1, tiled=T...  125 us
    reduce_scatter x1, waiting for transfers between devices, shards(): lax.psum_scatter(totals[1], ('blk', 'chan'), scatter_dimension=1, tiled=T...  104 us
    unnamed x3, blocking collectives  83.3 us
  transfers between devices with their start and end apart: 22, of which 13 were waited for; matrix products, arithmetic and copies ran while one was open for 9% of the time, Pallas kernels for 0%

commit v1 on v0

v1 whole, which is shorter than its diff:
```python
import math

import jax
import jax.numpy as jnp
from jax import lax
from jax.sharding import PartitionSpec as P

EPS = 1e-05
BANDS = 16
EXACT = lax.Precision.HIGHEST
AXES = ("blk", "chan")
F32 = jnp.float32
BF16 = jnp.bfloat16


def contract(a, b, dim_a, dim_b, precision=None):
    return lax.dot_general(
        a, b, (((dim_a,), (dim_b,)), ((), ())), precision=precision, preferred_element_type=F32
    )


def positions(length):
    lags = jnp.arange(length).astype(F32)
    band_freq = 0.0001 + (BANDS - 1 - 0.0001) * jnp.arange(BANDS).astype(F32) / (BANDS - 1)
    phase = 2.0 * math.pi / length * lags[None, :] * band_freq[:, None]
    return lags, jnp.concatenate([lags[None, :] / (length - 1), jnp.cos(phase), -jnp.sin(phase)], 0)


def filter_hidden(length, pos_weight, pos_bias, mid_weight, mid_bias, sine_freq):
    lags, features = positions(length)
    freq = sine_freq[:, None]
    first_sum = contract(pos_weight, features, 0, 0, EXACT) + pos_bias[:, None]
    first = jnp.sin(freq * first_sum)
    second_sum = contract(mid_weight, first, 0, 0, EXACT) + mid_bias[:, None]
    second = jnp.sin(freq * second_sum)
    return lags, features, first_sum, first, second_sum, second


def block_table(block):
    spot = lax.broadcasted_iota(jnp.int32, (block, block), 0)
    freq = lax.broadcasted_iota(jnp.int32, (block, block), 1)
    phase = (math.pi / block) * (spot * freq % (2 * block)).astype(F32)
    parity = 1.0 - 2.0 * (spot % 2).astype(F32)
    imag = jnp.where(freq == 0, parity, -jnp.sin(phase))
    return jnp.concatenate([jnp.cos(phase), imag], 1)


def to_spectrum(blocks, table):
    spec = lax.dot_general(
        blocks, table, (((blocks.ndim - 1,), (0,)), ((), ())), precision=EXACT, preferred_element_type=F32
    )
    half = table.shape[0]
    return spec[..., :half], spec[..., half:]


def from_spectrum(real, imag, table):
    half = table.shape[0]
    weight = jnp.where(lax.iota(jnp.int32, half) == 0, 0.5 / half, 1.0 / half)
    spec = jnp.concatenate([real * weight, imag * weight], -1)
    return lax.dot_general(
        spec, table, (((spec.ndim - 1,), (1,)), ((), ())), precision=EXACT, preferred_element_type=F32
    )


def packed_kernel(real, imag):
    first = lax.iota(jnp.int32, real.shape[-1]) == 0
    return real, jnp.where(first, imag, real), jnp.where(first, 0.0, imag)


def layer_norm(values, gain, shift):
    center = values - jnp.mean(values, -1, keepdims=True)
    scale_inv = lax.rsqrt(jnp.mean(center * center, -1, keepdims=True) + EPS)
    normal = center * scale_inv
    return normal * gain + shift, normal, scale_inv


def layer_norm_back(grad_out, normal, scale_inv, gain):
    grad_normal = grad_out * gain
    inner = grad_normal - jnp.mean(grad_normal, -1, keepdims=True)
    inner = inner - normal * jnp.mean(grad_normal * normal, -1, keepdims=True)
    return inner * scale_inv, jnp.sum(grad_out * normal, 0), jnp.sum(grad_out, 0)


def gelu_parts(v):
    root = math.sqrt(2.0 / math.pi)
    inner = root * (v + 0.044715 * v * v * v)
    t = jnp.tanh(inner)
    value = 0.5 * v * (1.0 + t)
    slope = 0.5 * (1.0 + t) + 0.5 * v * (1.0 - t * t) * root * (1.0 + 3.0 * 0.044715 * v * v)
    return value, slope


def delayed(values, steps):
    if steps == 0:
        return values
    pad = jnp.zeros(values.shape[:-1] + (steps,), values.dtype)
    return jnp.concatenate([pad, values[..., :-steps]], -1)


def advanced(values, steps):
    if steps == 0:
        return values
    pad = jnp.zeros(values.shape[:-1] + (steps,), values.dtype)
    return jnp.concatenate([values[..., steps:], pad], -1)


def exchange(values):
    return lax.all_to_all(values, AXES, split_axis=0, concat_axis=0, tiled=True)


def shards(
    hidden_in,
    cotangent,
    mixer_input_weight,
    mixer_output_weight,
    feedforward_up,
    feedforward_down,
    first_gain,
    first_shift,
    second_gain,
    second_shift,
    short_taps,
    short_bias,
    skip_scale,
    filter_out,
    pos_weight,
    pos_bias,
    mid_weight,
    mid_bias,
    sine_freq,
    decay_rate,
):
    devices = lax.axis_size(AXES)
    micro, seq_count, tok, width = hidden_in.shape
    seqs = micro * seq_count
    tokens = seqs * tok
    length = tok * devices
    chans = width // devices
    block = tok * lax.axis_size("chan")
    blocks = length // block

    def gather(shard):
        return lax.all_gather(shard, AXES, axis=0, tiled=True)

    rows_in, rows_out, rows_up = (w.shape[1] for w in (mixer_input_weight, mixer_output_weight, feedforward_up))
    weight_in = gather(mixer_input_weight.T)
    weight_out = gather(mixer_output_weight.T)
    weight_up = gather(feedforward_up.T)
    weight_down = gather(feedforward_down)
    norms = jnp.stack([first_gain, first_shift, second_gain, second_shift])
    norms = lax.all_gather(norms, AXES, axis=1, tiled=True).astype(F32)
    gain_one, shift_one, gain_two, shift_two = norms[0], norms[1], norms[2], norms[3]

    freq = sine_freq.astype(F32)
    w_pos, w_mid, w_fil = pos_weight.astype(F32), mid_weight.astype(F32), filter_out.astype(F32)
    lags, features, first_sum, first_act, second_sum, second_act = filter_hidden(
        length, w_pos, pos_bias.astype(F32), w_mid, mid_bias.astype(F32), freq
    )
    decay = jnp.exp(-lags[None, :] * decay_rate.astype(F32)[:, None])
    kernel = contract(w_fil, second_act, 0, 0, EXACT) * decay
    table = block_table(block)
    sign = 1.0 - 2.0 * (lax.iota(jnp.int32, block) % 2).astype(F32)
    ker_re, ker_im = to_spectrum(kernel.reshape(chans, blocks, block), table)

    def with_previous(spec):
        before = jnp.concatenate([jnp.zeros_like(spec[:, :1]), spec[:, :-1]], 1)
        return spec + sign * before

    k_re, k_alt, k_im = packed_kernel(with_previous(ker_re), with_previous(ker_im))

    values = hidden_in.reshape(tokens, width).astype(F32)
    normed, normal_one, inv_one = layer_norm(values, gain_one, shift_one)
    normed = normed.astype(BF16)
    projected = contract(weight_in, normed, 1, 1).astype(BF16)
    projected = projected.reshape(3, devices, chans, tokens).transpose(1, 0, 2, 3)
    arrived = exchange(projected)

    def by_sequence(values):
        parts = values.shape[1]
        values = values.reshape(devices, parts, chans, seqs, tok)
        return values.transpose(1, 3, 2, 0, 4).reshape(parts, seqs, chans, length)

    def by_device(values):
        parts = values.shape[0]
        values = values.reshape(parts, seqs, chans, devices, tok)
        return values.transpose(3, 0, 2, 1, 4).reshape(devices, parts, chans, tokens)

    steps = by_sequence(arrived).astype(F32)
    taps = short_taps.astype(F32)[:, :, None, :, None]
    conv = short_bias.astype(F32)[:, None, :, None]
    for i in range(3):
        conv = conv + taps[i] * delayed(steps, i)
    gate_out, gate_in, signal = conv[0], conv[1], conv[2]
    gated = signal * gate_in
    sig_re, sig_im = to_spectrum(gated.reshape(seqs, chans, blocks, block), table)

    def shifted_sum(make):
        total = None
        for d in range(blocks):
            term = make(d)
            total = term if total is None else tuple(a + b for a, b in zip(total, term))
        return total

    def ahead(x, d):
        return x if d == 0 else jnp.pad(x[:, :, :-d], ((0, 0), (0, 0), (d, 0), (0, 0)))

    def back(x, d):
        return x if d == 0 else jnp.pad(x[:, :, d:], ((0, 0), (0, 0), (0, d), (0, 0)))

    def forward_term(d):
        re, im = ahead(sig_re, d), ahead(sig_im, d)
        kr, ka, ki = k_re[:, d : d + 1], k_alt[:, d : d + 1], k_im[:, d : d + 1]
        return re * kr - im * ki, re * ki + im * ka

    out_re, out_im = shifted_sum(forward_term)
    long_out = from_spectrum(out_re, out_im, table).reshape(seqs, chans, length)
    skip = skip_scale.astype(F32)[None, :, None]
    long_total = long_out + skip * gated
    mixed = (long_total * gate_out).astype(BF16)
    mixed = exchange(by_device(mixed[None])).reshape(width, tokens)

    resid = values + contract(mixed, weight_out, 0, 1)
    second, normal_two, inv_two = layer_norm(resid, gain_two, shift_two)
    second = second.astype(BF16)
    upper = contract(second, weight_up, 1, 1)
    active, slope = gelu_parts(upper)
    active = active.astype(BF16)
    result = resid + contract(active, weight_down, 1, 0)

    cot = cotangent.reshape(tokens, width)
    grad_down = contract(active, cot, 0, 0)
    grad_upper = (contract(cot, weight_down, 1, 1) * slope).astype(BF16)
    grad_up = contract(grad_upper, second, 0, 0)
    grad_second = contract(grad_upper, weight_up, 1, 0)
    resid_term, grad_gain_two, grad_shift_two = layer_norm_back(grad_second, normal_two, inv_two, gain_two)
    grad_resid = cot.astype(F32) + resid_term
    grad_branch = grad_resid.astype(BF16)
    grad_out_w = contract(grad_branch, mixed, 0, 1)
    grad_mixed = contract(weight_out, grad_branch, 0, 1).astype(BF16)
    grad_mixed = exchange(grad_mixed.reshape(devices, 1, chans, tokens))
    grad_mixed = by_sequence(grad_mixed)[0].astype(F32)

    grad_gate_out = grad_mixed * long_total
    grad_long = grad_mixed * gate_out
    grad_skip = jnp.sum(grad_long * gated, (0, 2))
    gl_re, gl_im = to_spectrum(grad_long.reshape(seqs, chans, blocks, block), table)

    def signal_term(d):
        re, im = back(gl_re, d), back(gl_im, d)
        kr, ka, ki = k_re[:, d : d + 1], k_alt[:, d : d + 1], k_im[:, d : d + 1]
        return re * kr + im * ki, im * ka - re * ki

    gg_re, gg_im = shifted_sum(signal_term)
    grad_gated = from_spectrum(gg_re, gg_im, table).reshape(seqs, chans, length) + skip * grad_long

    first_slot = lax.iota(jnp.int32, block) == 0
    kg_re, kg_im = [], []
    for d in range(blocks):
        s_re, s_im = sig_re[:, :, : blocks - d], sig_im[:, :, : blocks - d]
        g_re, g_im = gl_re[:, :, d:], gl_im[:, :, d:]
        same, other = g_re * s_re, g_im * s_im
        kg_re.append(jnp.sum(jnp.where(first_slot, same, same + other), (0, 2)))
        kg_im.append(jnp.sum(jnp.where(first_slot, other, g_im * s_re - g_re * s_im), (0, 2)))
    kg_re, kg_im = jnp.stack(kg_re, 1), jnp.stack(kg_im, 1)

    def with_next(spec):
        after = jnp.concatenate([spec[:, 1:], jnp.zeros_like(spec[:, :1])], 1)
        return spec + sign * after

    grad_kernel = from_spectrum(with_next(kg_re), with_next(kg_im), table).reshape(chans, length)

    grad_conv = jnp.stack([grad_gate_out, grad_gated * signal, grad_gated * gate_in])
    grad_bias = jnp.sum(grad_conv, (1, 3))
    grad_taps = jnp.stack([jnp.sum(grad_conv * delayed(steps, i), (1, 3)) for i in range(3)])
    grad_steps = taps[0] * grad_conv
    for i in (1, 2):
        grad_steps = grad_steps + taps[i] * advanced(grad_conv, i)
    grad_proj = exchange(by_device(grad_steps.astype(BF16)))
    grad_proj = grad_proj.transpose(1, 0, 2, 3).reshape(3 * width, tokens)

    fade = grad_kernel * decay
    grad_filter = contract(second_act, fade, 1, 1, EXACT)
    grad_two = contract(w_fil, fade, 1, 0, EXACT) * jnp.cos(freq[:, None] * second_sum)
    grad_freq = jnp.sum(grad_two * second_sum, 1)
    grad_two = grad_two * freq[:, None]
    grad_mid = contract(first_act, grad_two, 1, 1, EXACT)
    grad_one = contract(w_mid, grad_two, 1, 0, EXACT) * jnp.cos(freq[:, None] * first_sum)
    grad_freq = grad_freq + jnp.sum(grad_one * first_sum, 1)
    grad_one = grad_one * freq[:, None]
    grad_pos = contract(features, grad_one, 1, 1, EXACT)
    small = lax.psum(
        jnp.concatenate([grad_pos, jnp.sum(grad_one, 1)[None], grad_mid, jnp.sum(grad_two, 1)[None], grad_freq[None]]),
        AXES,
    )
    emb, order = pos_weight.shape

    grad_in = contract(grad_proj, normed, 1, 0)
    grad_normed = contract(grad_proj, weight_in, 0, 0)
    input_term, grad_gain_one, grad_shift_one = layer_norm_back(grad_normed, normal_one, inv_one, gain_one)
    grad_hidden = (grad_resid + input_term).astype(BF16)

    def reduce_rows(partial):
        return lax.psum_scatter(partial.astype(BF16), AXES, scatter_dimension=0, tiled=True).astype(F32)

    norm_grads = jnp.stack([grad_gain_one, grad_shift_one, grad_gain_two, grad_shift_two])
    norm_grads = lax.psum_scatter(norm_grads, AXES, scatter_dimension=1, tiled=True)
    return (
        result.astype(BF16).reshape(hidden_in.shape),
        grad_hidden.reshape(hidden_in.shape),
        reduce_rows(grad_in).T,
        reduce_rows(grad_out_w).T,
        reduce_rows(grad_up).T,
        reduce_rows(grad_down),
        norm_grads[0],
        norm_grads[1],
        norm_grads[2],
        norm_grads[3],
        grad_taps,
        grad_bias,
        grad_skip,
        grad_filter,
        small[:emb],
        small[emb],
        small[emb + 1 : emb + 1 + order],
        small[emb + 1 + order],
        small[emb + 2 + order],
    )


def solution(mesh):
    rows, spread, tokens = P(AXES), P(None, AXES), P(None, None, AXES, None)
    params = (rows, rows, rows, rows, P(None, None, AXES), spread, rows, spread, P(), P(), P(), P(), P())
    return jax.shard_map(
        shards,
        mesh=mesh,
        in_specs=(tokens, tokens, spread, spread, spread, P(AXES, None)) + params + (rows,),
        out_specs=(tokens, tokens, spread, spread, spread, P(AXES, None)) + params,
        check_vma=False,
    )
```

time: 2070 us -> 728 us (0.35)
  blocking collectives: 660 us -> 83.1 us
  waiting for transfers between devices: 784 us -> 422 us
  matrix products: 242 us -> 63.1 us
  local copies, waits for them, and re-layouts: 152 us -> 74.8 us
  other arithmetic: 117 us -> 44.8 us
  loops' own time: 46.7 us -> 0 us
  starting transfers between devices: 37.1 us -> 14.3 us
    all_gather x11 -> x1, blocking collectives: 577 us -> 43.4 us  [shards(): norms = lax.all_gather(norms, AXES, axis=1, tiled=True).astype(F32)]
    unnamed x12 -> x8, waiting for transfers between devices: 250 us -> 2.63 us
    reduce_scatter x4, waiting for transfers between devices: 512 us -> 265 us  [reduce_rows(): lax.psum_scatter(partial.astype(BF16), AXES, scatter_dimension=0, tiled=T...]
    dot_general x170 -> x26, matrix products: 242 us -> 63.1 us  [the longest x20 55.4 us: contract(): lax.dot_general(a, b, (((dim_a,), (dim_b,)), ((), ())), precision=precisi...]
    all_gather x4, waiting for transfers between devices: 0.06 us -> 123 us  [gather(): return lax.all_gather(shard, AXES, axis=0, tiled=True)]
    another operation x52 -> x0, loops' own time: 46.7 us -> none  [the longest x2 21.6 us: visit_piece(): result, _ = lax.scan(visit_block, running, (indices,) + tuple(piece))]
    unnamed x3 -> x1, blocking collectives: 83.3 us -> 39.7 us
    dynamic_slice x54 -> x0, local copies, waits for them, and re-layouts: 41.6 us -> none  [the longest x50 40.6 us: visit_piece(): lax.scan(visit_block, running, (indices, piece[0], piece[1], piece[2]))]
  transfers between devices with their start and end apart: 22 -> 12, of which waited for: 13 -> 11; matrix products, arithmetic and copies ran while one was open for 9% -> 23% of each run, Pallas kernels for 0% -> 0%
where the time goes in v1:
time: 728 us; the launch traced here: 719 us
  waiting for transfers between devices  422 us (58%)
  blocking collectives  83.1 us (11%)
  local copies, waits for them, and re-layouts  74.8 us (10%)
  matrix products  63.1 us (9%)
  other arithmetic  44.8 us (6%)
  between operations  16.8 us (2%)
  starting transfers between devices  14.3 us (2%)
    reduce_scatter x4, waiting for transfers between devices, reduce_rows(): lax.psum_scatter(partial.astype(BF16), AXES, scatter_dimension=0, tiled=T...  265 us
    all_gather x4, waiting for transfers between devices, gather(): return lax.all_gather(shard, AXES, axis=0, tiled=True)  123 us
    dot_general x20, matrix products, contract(): lax.dot_general(a, b, (((dim_a,), (dim_b,)), ((), ())), precision=precisi...  55.4 us
    all_gather x1, blocking collectives, shards(): norms = lax.all_gather(norms, AXES, axis=1, tiled=True).astype(F32)  43.4 us
    unnamed x1, blocking collectives  39.7 us
    all_to_all x4, waiting for transfers between devices, exchange(): return lax.all_to_all(values, AXES, split_axis=0, concat_axis=0, tiled=True)  31 us
    unnamed x331, local copies, waits for them, and re-layouts  23.3 us
  transfers between devices with their start and end apart: 12, of which 11 were waited for; matrix products, arithmetic and copies ran while one was open for 23% of the time, Pallas kernels for 0%

profile of v1, /device:TPU:0, one launch (start us, length us, event | category | flops | bytes accessed | tf_op | source)
XLA Modules:
  0.0 719.1 jit_solution(14635279991504066053)
XLA Ops:
  13.0 43.4 %all-gather = bf16[32,24,4]{1,2,0:T(4,128)(2,1)S(1)} all-gather(bf16[1,24,4]{1,2,0:T(4,128)(2,1)S(1)} %maximum_bitcast_fusion), channel_id=1, replica_groups=mesh['blk'=8,'chan'=4] {'blk','chan'}, dimensions={0}, use_global_device_ids=true | all-gather | bytes 6336 | tf_op jit(solution)/shard_map/all_gather | solution.py:151
  62.6 2.2 fusion.6
  64.8 2.1 fusion.7
  71.0 2.8 all-gather.6.cloned.1.call-done
  73.7 3.3 fusion.1
  78.2 3.7 all-to-all-start
  96.5 3.0 all-to-all-done
  99.5 2.6 reshape.386
  102.1 1.4 copy-done.1
  103.5 2.1 copy.121
  105.6 2.2 reshape.381
  118.6 1.8 fusion.79
  121.6 1.9 reshape.368
  123.5 3.8 all-to-all-start.1
  127.3 3.1 all-gather.8.cloned.1.call-done
  130.4 5.8 all-to-all-done.1
  136.2 2.0 fusion.136
  138.4 57.5 %all-gather.10.cloned.1.call-done = bf16[3072,768]{1,0:T(8,128)(2,1)} async-done(((bf16[96,768]{1,0:T(8,128)(2,1)}), bf16[3072,768]{1,0:T(8,128)(2,1)}) %all-gather.10.cloned.1.call-update) | async-done | bytes 4718608 | tf_op jit(solution)/shard_map/all_gather | solution.py:143
  195.9 5.3 fusion.123
  201.2 60.0 %all-gather.12.cloned.1.call-done = bf16[3072,768]{1,0:T(8,128)(2,1)} async-done(((bf16[96,768]{1,0:T(8,128)(2,1)}), bf16[3072,768]{1,0:T(8,128)(2,1)}) %all-gather.12.cloned.1.call-update) | async-done | bytes 4718608 | tf_op jit(solution)/shard_map/all_gather | solution.py:143
  261.1 4.8 fusion
  265.9 1.5 multiply_reduce_fusion.6
  269.7 1.7 copy.124
  271.4 3.5 all-to-all-start.2
  275.0 1.8 reshape.373
  277.7 2.5 convolution_convert_fusion.4
  280.2 3.6 all-to-all-done.2
  283.9 2.3 reshape.387
  286.2 1.4 copy.126
  288.6 2.0 fusion.24
  297.2 1.4 fusion.64
  298.6 1.4 fusion.58
  300.0 2.2 reshape.382
  302.2 2.8 fusion.19
  304.9 1.8 reshape.374
  306.7 1.8 slice_multiply_fusion.2
  311.1 2.3 fusion.124
  313.4 2.3 reshape.375
  315.7 2.2 copy.128
  318.0 3.3 reshape.376
  321.3 2.7 all-to-all-start.3
  325.0 18.6 %all-to-all-done.3 = bf16[32,3,24,128]{3,2,1,0:T(8,128)(2,1)S(1)} async-done(((bf16[32,3,24,128]{3,2,1,0:T(8,128)(2,1)}), bf16[32,3,24,128]{3,2,1,0:T(8,128)(2,1)S(1)}, u32[]{:S(2)}, u32[]{:S(2)}) %all-to-all-start.3) | async-done | bytes 589856 | tf_op jit(solution)/shard_map/all_to_all | solution.py:108
  343.6 4.0 convolution_convert_fusion.2
  348.8 3.7 convolution_convert_fusion.1
  353.4 5.3 convolution_convert_fusion
  359.4 4.6 fusion.13
  365.3 2.3 stack.126
  372.9 2.0 fusion.5
  375.0 3.5 multiply_reduce_fusion.3
  378.8 1.6 copy.132
  380.4 1.6 copy.131
  382.0 1.5 copy.130
  384.2 2.3 fusion.35
  386.7 3.8 fusion.2
  391.2 1.7 fusion.84
  392.9 2.9 fusion.36
  396.8 39.7 %all-reduce.37 = (f32[4,768]{1,0:T(4,128)S(1)}, f32[100,64]{0,1:T(8,128)S(1)}) all-reduce(f32[4,768]{1,0:T(4,128)S(1)} %pad_maximum_fusion.11, f32[100,64]{0,1:T(8,128)S(1)} %concatenate.60), channel_id=6, replica_groups=mesh['blk'=8,'chan'=4] {'blk','chan'}, use_global_device_ids=true, to_apply=%region_16.17.clone | all-reduce | flops 9472 | bytes 75776
  440.2 1.4 convert_bitcast_fusion.2
  441.6 44.7 %reduce-scatter.6.cloned.1.call-done = bf16[72,768]{1,0:T(8,128)(2,1)} async-done(((bf16[2304,768]{1,0:T(8,128)(2,1)}), bf16[72,768]{1,0:T(8,128)(2,1)}) %reduce-scatter.6.cloned.1.call-update) | async-done | bytes 110608 | tf_op jit(solution)/shard_map/reduce_scatter | solution.py:303
  486.3 1.6 convert_bitcast_fusion.1
  487.9 109.8 %reduce-scatter.10.cloned.1.call-done = bf16[96,768]{1,0:T(8,128)(2,1)} async-done(((bf16[3072,768]{1,0:T(8,128)(2,1)}), bf16[96,768]{1,0:T(8,128)(2,1)}) %reduce-scatter.10.cloned.1.call-update) | async-done | bytes 147472 | tf_op jit(solution)/shard_map/reduce_scatter | solution.py:303
  597.7 1.6 convert_bitcast_fusion
  599.3 110.9 %reduce-scatter.12.cloned.1.call-done = bf16[96,768]{1,0:T(8,128)(2,1)} async-done(((bf16[3072,768]{1,0:T(8,128)(2,1)}), bf16[96,768]{1,0:T(8,128)(2,1)}) %reduce-scatter.12.cloned.1.call-update) | async-done | bytes 147472 | tf_op jit(solution)/shard_map/reduce_scatter | solution.py:303
  710.2 1.6 convert_element_type.304
  (469 shorter events, 72.3 us)
Async XLA Ops:
  7.2 55.4 %copy-start = (bf16[64,64]{1,0:T(8,128)(2,1)S(1)}, bf16[64,64]{1,0:T(8,128)(2,1)}, u32[]{:S(2)}) copy-start(bf16[64,64]{1,0:T(8,128)(2,1)} %param.36) | copy-start | bytes 24580
  7.2 66.5 %all-gather.6.cloned.1.call-start = ((), (), s32[]{:S(2)}) async-start(), calls=%async_computation.8 | async-start | bytes 3649536 | tf_op jit(solution)/shard_map/all_gather | solution.py:143
  7.9 122.4 %all-gather.8.cloned.1.call-start = ((), (), s32[]{:S(2)}) async-start(), calls=%async_computation.9 | async-start | bytes 1216512 | tf_op jit(solution)/shard_map/all_gather | solution.py:143
  8.7 187.2 %all-gather.10.cloned.1.call-start = ((), (), s32[]{:S(2)}) async-start(), calls=%async_computation.10 | async-start | bytes 4866048 | tf_op jit(solution)/shard_map/all_gather | solution.py:143
  8.7 56.0 %copy-start.119 = (bf16[64,24]{0,1:T(8,128)(2,1)S(1)}, bf16[64,24]{0,1:T(8,128)(2,1)}, u32[]{:S(2)}) copy-start(bf16[64,24]{0,1:T(8,128)(2,1)} %param.33) | copy-start | bytes 9220
  9.4 251.7 %all-gather.12.cloned.1.call-start = ((), (), s32[]{:S(2)}) async-start(), calls=%async_computation.11 | async-start | bytes 4866048 | tf_op jit(solution)/shard_map/all_gather | solution.py:143
  12.3 57.9 %copy-start.139 = (f32[128]{0:T(128)}, f32[128]{0:T(128)S(1)}, u32[]{:S(2)}) copy-start(f32[128]{0:T(128)S(1)} %div.40) | copy-start | bytes 1540
  12.3 54.6 %copy-start.106 = (f32[1,2048]{1,0:T(1,128)}, f32[1,2048]{1,0:T(1,128)S(1)}, u32[]{:S(2)}) copy-start(f32[1,2048]{1,0:T(1,128)S(1)} %convert_multiply_fusion.1) | copy-start | bytes 24580
  56.8 13.4 %copy-start.141 = (f32[128]{0:T(128)}, f32[128]{0:T(128)S(1)}, u32[]{:S(2)}) copy-start(f32[128]{0:T(128)S(1)} %rsqrt.21) | copy-start | bytes 1540
  60.2 6.8 copy-start.117
  60.8 6.1 copy-start.143
  61.4 6.2 copy-start.41
  61.4 6.2 copy-start.43
  62.6 7.8 %copy-start.17 = (f32[64,2048]{1,0:T(8,128)}, f32[64,2048]{1,0:T(8,128)S(1)}, u32[]{:S(2)}) copy-start(f32[64,2048]{1,0:T(8,128)S(1)} %fusion.3) | copy-start | bytes 1572868
  62.6 7.7 %copy-start.14 = (bf16[2,1,64,768]{3,2,1,0:T(8,128)(2,1)S(1)}, bf16[2,1,64,768]{3,2,1,0:T(8,128)(2,1)}, u32[]{:S(2)}) copy-start(bf16[2,1,64,768]{3,2,1,0:T(8,128)(2,1)} %param.20) | copy-start | bytes 589828
  64.8 6.2 copy-start.5
  67.0 15.0 %copy-start.108 = (pred[256]{0:T(512)(128)(4,1)}, pred[256]{0:T(512)(128)(4,1)S(1)}, u32[]{:S(2)}) copy-start(pred[256]{0:T(512)(128)(4,1)S(1)} %get-tuple-element.236) | copy-start | bytes 772
  67.6 14.4 %copy-start.133 = (f32[256]{0:T(256)}, f32[256]{0:T(256)S(1)}, u32[]{:S(2)}) copy-start(f32[256]{0:T(256)S(1)} %get-tuple-element.239) | copy-start | bytes 3076
  68.2 8.8 %copy-start.111 = (f32[768]{0:T(1024)}, f32[768]{0:T(1024)S(1)}, u32[]{:S(2)}) copy-start(f32[768]{0:T(1024)S(1)} %get-tuple-element.150) | copy-start | bytes 9220
  70.2 46.5 %copy-start.8 = (f32[256,256]{1,0:T(8,128)}, f32[256,256]{1,0:T(8,128)S(1)}, u32[]{:S(2)}) copy-start(f32[256,256]{1,0:T(8,128)S(1)} %negate_select_fusion.2) | copy-start | bytes 786436
  78.2 21.3 %all-to-all-start = ((bf16[32,3,24,128]{3,2,1,0:T(8,128)(2,1)}), bf16[32,3,24,128]{3,2,1,0:T(8,128)(2,1)}, u32[]{:S(2)}, u32[]{:S(2)}) async-start(bf16[32,3,24,128]{3,2,1,0:T(8,128)(2,1)} %copy.120), calls=%async_computation | async-start | bytes 1179648 | tf_op jit(solution)/shard_map/all_to_all | solution.py:108
  82.0 13.9 %copy-start.149 = (bf16[24]{0:T(256)(128)(2,1)S(1)}, bf16[24]{0:T(256)(128)(2,1)}, u32[]{:S(2)}) copy-start(bf16[24]{0:T(256)(128)(2,1)} %param.32) | copy-start | bytes 148
  96.5 11.3 %copy-start.121 = (f32[3,24]{1,0:T(4,128)}, f32[3,24]{1,0:T(4,128)S(1)}, u32[]{:S(2)}) copy-start(f32[3,24]{1,0:T(4,128)S(1)} %get-tuple-element.219) | copy-start | bytes 868
  96.5 11.4 %copy-start.123 = (f32[3,24]{1,0:T(4,128)}, f32[3,24]{1,0:T(4,128)S(1)}, u32[]{:S(2)}) copy-start(f32[3,24]{1,0:T(4,128)S(1)} %get-tuple-element.220) | copy-start | bytes 868
  96.5 11.4 %copy-start.125 = (f32[3,24]{1,0:T(4,128)}, f32[3,24]{1,0:T(4,128)S(1)}, u32[]{:S(2)}) copy-start(f32[3,24]{1,0:T(4,128)S(1)} %get-tuple-element.221) | copy-start | bytes 868
  123.5 12.7 %all-to-all-start.1 = ((bf16[32,1,24,128]{3,2,1,0:T(8,128)(2,1)}), bf16[32,1,24,128]{3,2,1,0:T(8,128)(2,1)S(1)}, u32[]{:S(2)}, u32[]{:S(2)}) async-start(bf16[32,1,24,128]{3,2,1,0:T(8,128)(2,1)} %bitcast.23), calls=%async_computation.1 | async-start | bytes 393216 | tf_op jit(solution)/shard_map/all_to_all | solution.py:108
  136.2 65.0 %copy-start.39 = (bf16[32,1,24,128]{3,2,1,0:T(8,128)(2,1)}, bf16[32,1,24,128]{3,2,1,0:T(8,128)(2,1)S(1)}, u32[]{:S(2)}) copy-start(bf16[32,1,24,128]{3,2,1,0:T(8,128)(2,1)S(1)} %all-to-all-done.1) | copy-start | bytes 589828
  138.2 129.3 %copy-start.129 = (f32[128]{0:T(128)}, f32[128]{0:T(128)S(1)}, u32[]{:S(2)}) copy-start(f32[128]{0:T(128)S(1)} %broadcast_multiply_fusion.5) | copy-start | bytes 1540
  138.4 129.1 %copy-start.135 = (f32[128]{0:T(128)}, f32[128]{0:T(128)S(1)}, u32[]{:S(2)}) copy-start(f32[128]{0:T(128)S(1)} %add_rsqrt_fusion.1) | copy-start | bytes 1540
  195.9 65.2 %copy-start.45 = (bf16[2,1,64,768]{3,2,1,0:T(8,128)(2,1)S(1)}, bf16[2,1,64,768]{3,2,1,0:T(8,128)(2,1)}, u32[]{:S(2)}) copy-start(bf16[2,1,64,768]{3,2,1,0:T(8,128)(2,1)} %param.21) | copy-start | bytes 589828
  261.1 4.8 copy-start.3
  268.7 9.1 %copy-start.22 = (f32[128,768]{1,0:T(8,128)}, f32[128,768]{1,0:T(8,128)S(1)}, u32[]{:S(2)}) copy-start(f32[128,768]{1,0:T(8,128)S(1)} %multiply_add_fusion.3) | copy-start | bytes 1179652
  271.4 12.4 %all-to-all-start.2 = ((bf16[32,1,24,128]{3,2,1,0:T(8,128)(2,1)}), bf16[32,1,24,128]{3,2,1,0:T(8,128)(2,1)}, u32[]{:S(2)}, u32[]{:S(2)}) async-start(bf16[32,1,24,128]{3,2,1,0:T(8,128)(2,1)} %bitcast.300), calls=%async_computation.2 | async-start | bytes 393216 | tf_op jit(solution)/shard_map/all_to_all | solution.py:108
  275.0 165.2 %reduce-scatter.8.cloned.1.call-start = ((), (), s32[]{:S(2)}) async-start(), calls=%async_computation.13 | async-start | bytes 1216512 | tf_op jit(solution)/shard_map/reduce_scatter | solution.py:303
  300.0 6.8 copy-start.148
  318.0 6.1 copy-start.15
  318.0 6.1 copy-start.112
  318.0 6.1 copy-start.132
  318.0 6.1 copy-start.147
  321.3 22.2 %all-to-all-start.3 = ((bf16[32,3,24,128]{3,2,1,0:T(8,128)(2,1)}), bf16[32,3,24,128]{3,2,1,0:T(8,128)(2,1)S(1)}, u32[]{:S(2)}, u32[]{:S(2)}) async-start(bf16[32,3,24,128]{3,2,1,0:T(8,128)(2,1)} %reshape.376), calls=%async_computation.3 | async-start | bytes 1179648 | tf_op jit(solution)/shard_map/all_to_all | solution.py:108
  324.0 162.2 %reduce-scatter.6.cloned.1.call-start = ((), (), s32[]{:S(2)}) async-start(), calls=%async_computation.12 | async-start | bytes 3649536 | tf_op jit(solution)/shard_map/reduce_scatter | solution.py:303
  343.6 4.1 copy-start.29
  347.7 250.0 %reduce-scatter.10.cloned.1.call-start = ((), (), s32[]{:S(2)}) async-start(), calls=%async_computation.14 | async-start | bytes 4866048 | tf_op jit(solution)/shard_map/reduce_scatter | solution.py:303
  352.5 357.6 %reduce-scatter.12.cloned.1.call-start = ((), (), s32[]{:S(2)}) async-start(), calls=%async_computation.15 | async-start | bytes 4866048 | tf_op jit(solution)/shard_map/reduce_scatter | solution.py:303
  359.4 4.6 copy-start.25
  364.0 3.6 copy-start.27
  364.0 4.9 copy-start.11
  365.3 4.6 copy-start.110
  372.9 5.8 copy-start.35
  375.0 5.4 copy-start.36
  380.4 3.8 copy-start.19
  380.4 3.8 copy-start.33
  382.0 4.6 copy-start.2
  386.7 3.9 copy-start.137
  386.7 3.9 copy-start.138
  386.7 4.5 copy-start.13
  386.7 4.5 copy-start.40
  386.7 6.3 copy-start.145
  386.7 9.1 %copy-start.4 = (bf16[2304,768]{1,0:T(8,128)(2,1)S(1)}, bf16[2304,768]{1,0:T(8,128)(2,1)}, u32[]{:S(2)}) copy-start(bf16[2304,768]{1,0:T(8,128)(2,1)} %all-gather.6.cloned.1.call-done) | copy-start | bytes 10616836
  390.6 5.3 copy-start.16
  390.6 5.3 copy-start.30
  390.6 5.3 copy-start.140
  390.6 5.3 copy-start.142
  395.9 43.4 %copy-start.23 = (f32[128,768]{1,0:T(8,128)S(1)}, f32[128,768]{1,0:T(8,128)}, u32[]{:S(2)}) copy-start(f32[128,768]{1,0:T(8,128)} %copy-done.22) | copy-start | bytes 1179652
  (98 other events, 133.0 us)
Sparse Core Ops, SparseCore 0:
  10.9 62.7 all-gather.5
  76.6 53.7 all-gather.7
  133.3 62.5 all-gather.9
  198.7 62.4 all-gather.11
  280.6 98.2 reduce-scatter.7
  384.1 102.0 reduce-scatter.5
  491.7 105.8 reduce-scatter.9
  604.0 106.0 reduce-scatter.11
